TPU v7x, 32 devices: a whole 2x2x4 slice. The times are simulated.
32 devices in a mesh: dp: 4 (over y, core), fsdp: 8 (over z, x).
Axes of the slice: x: 2, y: 2, z: 4, core: 2. Of those that a mesh axis runs over, the one named last changes fastest.
Arguments:
- tokens: bfloat16 [4096, 1536], P(('dp', 'fsdp')), may hold values from -6 to 6
- seq_ids: int32 [32, 128], P(('dp', 'fsdp')), may hold values from 0 to 127, as said below
- routes: int32 [4096, 8], P(('dp', 'fsdp')), may hold values from 0 to 39, all different within a row; in each aligned block of 128 rows (0 to 127, 128 to 255, ...) at most 32 rows name the same one
- cotangent: bfloat16 [4096, 1536], P(('dp', 'fsdp')), may hold values from -6 to 6
- gain_attn: bfloat16 [1536], P(('dp', 'fsdp')), may hold values from 0.5 to 1.5
- qkv_weight: bfloat16 [1536, 2560], P(('dp', 'fsdp')), may hold values from -0.15625 to 0.15625
- out_weight: bfloat16 [1536, 1536], P(('dp', 'fsdp')), may hold values from -0.625 to 0.625
- gain_moe: bfloat16 [1536], P(('dp', 'fsdp')), may hold values from 0.5 to 1.5
- router_weight: bfloat16 [1536, 40], P(('dp', 'fsdp')), may hold values from -0.3125 to 0.3125
- expert_weight: bfloat16 [40, 1536, 1536], P('dp', 'fsdp'), may hold values from -0.3125 to 0.3125
Outputs:
- block_out: bfloat16 [4096, 1536], P(('dp', 'fsdp'))
- d_tokens: float32 [4096, 1536], P(('dp', 'fsdp'))
- d_gain_attn: float32 [1536], P(('dp', 'fsdp'))
- d_qkv_weight: float32 [1536, 2560], P(('dp', 'fsdp'))
- d_out_weight: float32 [1536, 1536], P(('dp', 'fsdp'))
- d_gain_moe: float32 [1536], P(('dp', 'fsdp'))
- d_router_weight: float32 [1536, 40], P(('dp', 'fsdp'))
- d_expert_weight: float32 [40, 1536, 1536], P('dp', 'fsdp')
Inputs may be any that keep to these rules, and one draw needn't show every extreme that they name: `routes`: in each device's 128 rows no expert is named more than 32 times, a bound that some block reaches. `seq_ids`: within each row the ids start at 0 and rise by 0 or 1 from slot to slot; every sequence has 1 to 128 tokens; some row holds a single sequence of 128 tokens, and some row holds 128 sequences of one token.
All inputs are finite; a program needn't handle non-finite values.
Results may differ from a plain program's by a relative error of at most 0.018.
Values may be sent and summed in bfloat16 or wider, within the bound.
No kernel may reach another device: no remote copies, remote signals or barrier semaphores. Data moves between devices by JAX's collectives and lax.ppermute only.
A program may use at most 384 MiB of HBM per device.

v0:
```python
import jax
import jax.numpy as jnp
from jax import lax
from jax.sharding import PartitionSpec as P

D = 1536
H = 24
KV = 8
HD = 64
E = 40
CAP = 32


norm_eps = 1e-06


def rope_tables(seq_row, half_width):
    length = seq_row.shape[0]
    places = jnp.arange(length)
    same_seq = seq_row[:, None] == seq_row[None, :]
    earlier = places[None, :] < places[:, None]
    position = jnp.sum(jnp.where(same_seq & earlier, 1, 0), axis=1).astype(jnp.int32)
    inverse = 10000.0 ** (-jnp.arange(half_width).astype(jnp.float32) / half_width)
    angles = position.astype(jnp.float32)[:, None] * inverse[None, :]
    visible = same_seq & (places[None, :] <= places[:, None])
    return (jnp.cos(angles), jnp.sin(angles), visible)


def rotate(values, cosine, sine_table):
    half_width = values.shape[-1] // 2
    first_half = values[..., :half_width]
    second_half = values[..., half_width:]
    cos_wide = cosine[:, None, :]
    sin_wide = sine_table[:, None, :]
    return jnp.concatenate(
        [
            first_half * cos_wide - second_half * sin_wide,
            second_half * cos_wide + first_half * sin_wide,
        ],
        axis=-1,
    )


def unrotate(grad_rows, cosine, sine_table):
    half_width = grad_rows.shape[-1] // 2
    first_half = grad_rows[..., :half_width]
    second_half = grad_rows[..., half_width:]
    cos_wide = cosine[:, None, :]
    sin_wide = sine_table[:, None, :]
    return jnp.concatenate(
        [
            first_half * cos_wide + second_half * sin_wide,
            second_half * cos_wide - first_half * sin_wide,
        ],
        axis=-1,
    )


def norm_forward(values, gain_vec):
    inv_rms = lax.rsqrt(jnp.mean(values * values, axis=-1, keepdims=True) + norm_eps)
    return (inv_rms, values * inv_rms * gain_vec.astype(jnp.float32))


def norm_backward(values, inv_rms, gain_vec, upstream):
    weighted = upstream * gain_vec.astype(jnp.float32)
    d_gain = jnp.sum(upstream * values * inv_rms, axis=0)
    d_values = inv_rms * (
        weighted - values * inv_rms * inv_rms * jnp.mean(weighted * values, axis=-1, keepdims=True)
    )
    return (d_values, d_gain)


def attend_group(group_in, visible, factor):
    queries, keys_rot, values_in = group_in
    scores = (
        jnp.einsum("gqd,kd->gqk", queries, keys_rot, preferred_element_type=jnp.float32) * factor
    )
    exp_scores = jnp.where(visible[None], jnp.exp(scores), 0.0)
    totals = jnp.sum(exp_scores, axis=-1)
    attn_probs = (exp_scores / totals[..., None]).astype(jnp.bfloat16)
    mixed_heads = jnp.einsum(
        "gqk,kd->gqd", attn_probs, values_in, preferred_element_type=jnp.float32
    )
    return (mixed_heads.astype(jnp.bfloat16), jnp.log(totals))


def attend_back(group_in, visible, factor):
    queries, keys_rot, values_in, mixed_heads, log_totals, d_mixed = group_in
    scores = (
        jnp.einsum("gqd,kd->gqk", queries, keys_rot, preferred_element_type=jnp.float32) * factor
    )
    recomputed = jnp.where(visible[None], jnp.exp(scores - log_totals[..., None]), 0.0)
    row_delta = jnp.sum(d_mixed.astype(jnp.float32) * mixed_heads.astype(jnp.float32), axis=-1)
    d_probs = jnp.einsum("gqd,kd->gqk", d_mixed, values_in, preferred_element_type=jnp.float32)
    d_scores = (recomputed * (d_probs - row_delta[..., None])).astype(jnp.bfloat16)
    d_query = (
        jnp.einsum("gqk,kd->gqd", d_scores, keys_rot, preferred_element_type=jnp.float32) * factor
    )
    d_keys = (
        jnp.einsum("gqk,gqd->kd", d_scores, queries, preferred_element_type=jnp.float32) * factor
    )
    d_values = jnp.einsum(
        "gqk,gqd->kd", recomputed.astype(jnp.bfloat16), d_mixed, preferred_element_type=jnp.float32
    )
    return (d_query, d_keys, d_values)


def dispatch_plan(route_row, experts, capacity):
    flat_routes = route_row.reshape(-1)
    pair_count = flat_routes.shape[0]
    hit_table = (flat_routes[:, None] == jnp.arange(experts)[None, :]).astype(jnp.int32)
    earlier = jnp.cumsum(hit_table, axis=0) - hit_table
    slot_index = jnp.sum(earlier * hit_table, axis=1)
    places = flat_routes * capacity + slot_index
    source = (
        jnp.full((experts * capacity,), pair_count, jnp.int32)
        .at[places]
        .set(jnp.arange(pair_count))
    )
    return (places, source)


def expert_out(block_rows, weight):
    hidden_width = weight.shape[-1] // 3
    both_parts = jnp.einsum(
        "secd,edf->secf",
        block_rows,
        weight[..., : 2 * hidden_width],
        preferred_element_type=jnp.float32,
    )
    gate_part = both_parts[..., :hidden_width]
    up_part = both_parts[..., hidden_width:]
    hidden = (gate_part * jax.nn.sigmoid(gate_part) * up_part).astype(jnp.bfloat16)
    return jnp.einsum(
        "secf,edf->secd",
        hidden,
        weight[..., 2 * hidden_width :],
        preferred_element_type=jnp.float32,
    ).astype(jnp.bfloat16)


def expert_back(block_rows, block_grads, weight):
    hidden_width = weight.shape[-1] // 3
    up_proj = weight[..., : 2 * hidden_width]
    both_parts = jnp.einsum(
        "secd,edf->secf", block_rows, up_proj, preferred_element_type=jnp.float32
    )
    gate_part = both_parts[..., :hidden_width]
    up_part = both_parts[..., hidden_width:]
    sigmoid_gate = jax.nn.sigmoid(gate_part)
    hidden = (gate_part * sigmoid_gate * up_part).astype(jnp.bfloat16)
    d_hidden = jnp.einsum(
        "secd,edf->secf",
        block_grads,
        weight[..., 2 * hidden_width :],
        preferred_element_type=jnp.float32,
    )
    d_both = jnp.concatenate(
        [
            d_hidden * up_part * sigmoid_gate * (1.0 + gate_part * (1.0 - sigmoid_gate)),
            d_hidden * gate_part * sigmoid_gate,
        ],
        axis=-1,
    ).astype(jnp.bfloat16)
    d_input = jnp.einsum(
        "secf,edf->secd", d_both, up_proj, preferred_element_type=jnp.float32
    ).astype(jnp.bfloat16)
    return (d_input, d_both, hidden)


def grad_terms(block_rows, block_grads, d_both, hidden):
    first_term = jnp.einsum(
        "secd,secf->edf", block_rows, d_both, preferred_element_type=jnp.float32
    )
    second_term = jnp.einsum(
        "secd,secf->edf", block_grads, hidden, preferred_element_type=jnp.float32
    )
    return jnp.concatenate([first_term, second_term], axis=-1)


def fetch_dense(gain_attn, qkv_weight, out_weight, gain_moe, router_weight):
    return (
        lax.all_gather(gain_attn, ("dp", "fsdp"), axis=0, tiled=True),
        lax.all_gather(qkv_weight, ("dp", "fsdp"), axis=0, tiled=True),
        lax.all_gather(out_weight, ("dp", "fsdp"), axis=0, tiled=True),
        lax.all_gather(gain_moe, ("dp", "fsdp"), axis=0, tiled=True),
        lax.all_gather(router_weight, ("dp", "fsdp"), axis=0, tiled=True),
    )


def fetch_experts(expert_weight):
    return lax.all_gather(expert_weight, "fsdp", axis=1, tiled=True)


def on_device(
    tokens,
    seq_ids,
    routes,
    cotangent,
    gain_attn,
    qkv_weight,
    out_weight,
    gain_moe,
    router_weight,
    expert_weight,
):
    length = tokens.shape[0]
    top_count = routes.shape[1]
    dp_count = lax.axis_size("dp")
    local_count = expert_weight.shape[0]
    query_width = H * HD
    kv_width = KV * HD
    group_size = H // KV
    factor = HD ** (-0.5)
    dense_full = fetch_dense(gain_attn, qkv_weight, out_weight, gain_moe, router_weight)
    held_experts = fetch_experts(expert_weight)
    gain_one, qkv_full, out_full, gain_two, router_full = dense_full
    cosine, sine_table, visible = rope_tables(seq_ids[0], HD // 2)
    stream_in = tokens.astype(jnp.float32)
    inv_one, normed = norm_forward(stream_in, gain_one)
    normed_one = normed.astype(jnp.bfloat16)
    qkv_proj = jnp.dot(normed_one, qkv_full, preferred_element_type=jnp.float32)
    queries = rotate(qkv_proj[:, :query_width].reshape(length, H, HD), cosine, sine_table).astype(
        jnp.bfloat16
    )
    keys_rot = rotate(
        qkv_proj[:, query_width : query_width + kv_width].reshape(length, KV, HD),
        cosine,
        sine_table,
    ).astype(jnp.bfloat16)
    values_in = qkv_proj[:, query_width + kv_width :].reshape(length, KV, HD).astype(jnp.bfloat16)
    query_groups = queries.reshape(length, KV, group_size, HD).transpose(1, 2, 0, 3)
    key_groups = keys_rot.transpose(1, 0, 2)
    value_groups = values_in.transpose(1, 0, 2)

    def forward_group(group_in):
        return attend_group(group_in, visible, factor)

    mixed_groups, log_totals = lax.map(forward_group, (query_groups, key_groups, value_groups))
    mixed_flat = mixed_groups.transpose(2, 0, 1, 3).reshape(length, query_width)
    resid_mid = stream_in + jnp.dot(mixed_flat, out_full, preferred_element_type=jnp.float32)
    inv_two, normed = norm_forward(resid_mid, gain_two)
    normed_two = normed.astype(jnp.bfloat16)
    logits = jnp.dot(normed_two, router_full, preferred_element_type=jnp.float32)
    chosen = routes[:, :, None] == jnp.arange(E)[None, None, :]
    picked = jnp.sum(jnp.where(chosen, logits[:, None, :], 0.0), axis=-1)
    exp_picked = jnp.exp(picked)
    gate_probs = exp_picked / jnp.sum(exp_picked, axis=-1, keepdims=True)
    places, source = dispatch_plan(routes, E, CAP)
    token_of = source // top_count
    padded_rows = jnp.concatenate([normed_two, jnp.zeros((1, D), jnp.bfloat16)], axis=0)
    slot_rows = padded_rows[token_of].reshape(E, CAP, D)
    owner_blocks = slot_rows.reshape(dp_count, local_count, CAP, D)
    owner_out = expert_out(
        lax.all_to_all(owner_blocks, "dp", split_axis=0, concat_axis=0, tiled=True), held_experts
    )
    expert_result = lax.all_to_all(
        owner_out, "dp", split_axis=0, concat_axis=0, tiled=True
    ).reshape(E, CAP, D)
    gathered = (
        expert_result.reshape(E * CAP, D)[places].reshape(length, top_count, D).astype(jnp.float32)
    )
    expert_sum = jnp.sum(gate_probs[:, :, None] * gathered, axis=1)
    block_out = (resid_mid + expert_sum).astype(jnp.bfloat16)
    dense_back = fetch_dense(gain_attn, qkv_weight, out_weight, gain_moe, router_weight)
    experts_back = fetch_experts(expert_weight)
    gain_one_back, qkv_back, out_back, gain_two_back, router_back = dense_back
    d_block = cotangent.astype(jnp.float32)
    d_gates = jnp.sum(gathered * d_block[:, None, :], axis=-1)
    d_picked = gate_probs * (d_gates - jnp.sum(gate_probs * d_gates, axis=-1, keepdims=True))
    d_logits = jnp.sum(jnp.where(chosen, d_picked[:, :, None], 0.0), axis=1).astype(jnp.bfloat16)
    gate_padded = jnp.concatenate([gate_probs.reshape(-1), jnp.zeros((1,), jnp.float32)])
    block_padded = jnp.concatenate([d_block, jnp.zeros((1, D), jnp.float32)], axis=0)
    d_slots = (
        (gate_padded[source][:, None] * block_padded[token_of])
        .astype(jnp.bfloat16)
        .reshape(E, CAP, D)
    )
    owner_grads = d_slots.reshape(dp_count, local_count, CAP, D)
    block_rows = lax.all_to_all(owner_blocks, "dp", split_axis=0, concat_axis=0, tiled=True)
    block_grads = lax.all_to_all(owner_grads, "dp", split_axis=0, concat_axis=0, tiled=True)
    d_input, d_both, hidden = expert_back(block_rows, block_grads, experts_back)
    d_input, d_both, hidden, got_rows, got_grads = (
        d_input,
        d_both,
        hidden,
        block_rows,
        block_grads,
    )
    d_expert_in = lax.all_to_all(d_input, "dp", split_axis=0, concat_axis=0, tiled=True).reshape(
        E, CAP, D
    )
    expert_term = grad_terms(got_rows, got_grads, d_both, hidden)
    d_expert_weight = lax.psum_scatter(
        expert_term.astype(jnp.bfloat16), "fsdp", scatter_dimension=1, tiled=True
    ).astype(jnp.float32)
    d_normed_two = jnp.sum(
        d_expert_in.reshape(E * CAP, D)[places].reshape(length, top_count, D).astype(jnp.float32),
        axis=1,
    )
    d_normed_two = d_normed_two + jnp.dot(
        d_logits, router_back.T, preferred_element_type=jnp.float32
    )
    d_router = jnp.dot(normed_two.T, d_logits, preferred_element_type=jnp.float32)
    d_resid, d_gain_two = norm_backward(resid_mid, inv_two, gain_two_back, d_normed_two)
    d_resid = d_resid + d_block
    d_resid_half = d_resid.astype(jnp.bfloat16)
    d_out = jnp.dot(mixed_flat.T, d_resid_half, preferred_element_type=jnp.float32)
    d_mixed = jnp.dot(d_resid_half, out_back.T, preferred_element_type=jnp.float32).astype(
        jnp.bfloat16
    )
    d_mixed_groups = d_mixed.reshape(length, KV, group_size, HD).transpose(1, 2, 0, 3)

    def backward_group(group_in):
        return attend_back(group_in, visible, factor)

    d_query, d_keys, d_values = lax.map(
        backward_group,
        (query_groups, key_groups, value_groups, mixed_groups, log_totals, d_mixed_groups),
    )
    d_query = unrotate(d_query.transpose(2, 0, 1, 3).reshape(length, H, HD), cosine, sine_table)
    d_keys = unrotate(d_keys.transpose(1, 0, 2), cosine, sine_table)
    d_qkv_act = jnp.concatenate(
        [
            d_query.reshape(length, query_width),
            d_keys.reshape(length, kv_width),
            d_values.transpose(1, 0, 2).reshape(length, kv_width),
        ],
        axis=-1,
    ).astype(jnp.bfloat16)
    d_qkv = jnp.dot(normed_one.T, d_qkv_act, preferred_element_type=jnp.float32)
    d_normed_one = jnp.dot(d_qkv_act, qkv_back.T, preferred_element_type=jnp.float32)
    d_stream, d_gain_one = norm_backward(stream_in, inv_one, gain_one_back, d_normed_one)
    d_tokens = d_stream + d_resid
    d_gain_attn, d_qkv_weight, d_out_weight, d_gain_moe, d_router_weight = (
        lax.psum_scatter(d_gain_one, ("dp", "fsdp"), scatter_dimension=0, tiled=True),
        lax.psum_scatter(d_qkv, ("dp", "fsdp"), scatter_dimension=0, tiled=True),
        lax.psum_scatter(d_out, ("dp", "fsdp"), scatter_dimension=0, tiled=True),
        lax.psum_scatter(d_gain_two, ("dp", "fsdp"), scatter_dimension=0, tiled=True),
        lax.psum_scatter(d_router, ("dp", "fsdp"), scatter_dimension=0, tiled=True),
    )
    return (
        block_out,
        d_tokens,
        d_gain_attn,
        d_qkv_weight,
        d_out_weight,
        d_gain_moe,
        d_router_weight,
        d_expert_weight,
    )


def solution(mesh):
    in_specs = (
        P(("dp", "fsdp"), None),
        P(("dp", "fsdp"), None),
        P(("dp", "fsdp"), None),
        P(("dp", "fsdp"), None),
        P(("dp", "fsdp")),
        P(("dp", "fsdp"), None),
        P(("dp", "fsdp"), None),
        P(("dp", "fsdp")),
        P(("dp", "fsdp"), None),
        P("dp", "fsdp", None),
    )
    out_specs = (
        P(("dp", "fsdp"), None),
        P(("dp", "fsdp"), None),
        P(("dp", "fsdp")),
        P(("dp", "fsdp"), None),
        P(("dp", "fsdp"), None),
        P(("dp", "fsdp")),
        P(("dp", "fsdp"), None),
        P("dp", "fsdp", None),
    )
    return jax.shard_map(
        on_device, mesh=mesh, in_specs=in_specs, out_specs=out_specs, check_vma=False
    )
```

profile of v0, /device:TPU:0, one launch (start us, length us, event | category | flops | bytes accessed | tf_op | source)
XLA Modules:
  0.0 2395.4 jit_solution(15239843079377520675)
XLA Ops:
  10.5 43.3 %all-reduce.7 = (bf16[1536]{0:T(1024)(128)(2,1)S(1)}, bf16[1536]{0:T(1024)(128)(2,1)S(1)}) all-reduce(bf16[1536]{0:T(1024)(128)(2,1)S(1)} %dynamic-update-slice, bf16[1536]{0:T(1024)(128)(2,1)S(1)} %dynamic-update-slice.1), channel_id=1, replica_groups=mesh['dp'=4,'fsdp'=8] {'dp','fsdp'}, use_global_device_ids=true, to_apply=%add.2 | all-reduce | flops 3072 | bytes 12288
  54.0 11.3 reduce-window.6
  70.6 18.6 all-gather.5.cloned.1.call-done
  103.6 50.7 %all-gather.7.cloned.1.call-done = bf16[1536,1536]{1,0:T(8,128)(2,1)} async-done(((bf16[48,1536]{1,0:T(8,128)(2,1)}), bf16[1536,1536]{1,0:T(8,128)(2,1)}) %all-gather.7.cloned.1.call-update) | async-done | bytes 4718608 | tf_op jit(solution)/shard_map/all_gather | solution.py:185
  169.3 145.3 %all-gather = bf16[32,48,40]{1,2,0:T(8,128)(2,1)S(1)} all-gather(bf16[1,48,40]{1,2,0:T(8,128)(2,1)S(1)} %bitcast.270), channel_id=1, replica_groups=mesh['dp'=4,'fsdp'=8] {'dp','fsdp'}, dimensions={0}, use_global_device_ids=true | all-gather | bytes 126720 | tf_op jit(solution)/shard_map/all_gather | solution.py:187
  341.0 713.3 %all-gather.9.cloned.1.call-done = bf16[10,1536,1536]{2,1,0:T(8,128)(2,1)} async-done(((bf16[10,192,1536]{2,1,0:T(8,128)(2,1)}), bf16[10,1536,1536]{2,1,0:T(8,128)(2,1)}) %all-gather.9.cloned.1.call-update) | async-done | bytes 47185936 | tf_op jit(solution)/shard_map/all_gather | solution.py:192
  1054.3 15.8 fusion.70
  1070.1 10.8 fusion.66
  1080.9 13.0 fusion.62
  1113.5 15.6 bitcast_convert_fusion
  1129.1 19.5 all-to-all-done.1
  1164.8 33.6 %pad_maximum_fusion = bf16[10,1536,1536]{1,2,0:T(8,128)(2,1)} fusion(bf16[10,1536,512]{1,2,0:T(8,128)(2,1)} %bitcast_convert_fusion.1, bf16[10,1536,1024]{1,2,0:T(8,128)(2,1)} %bitcast_convert_fusion), kind=kLoop, calls=%fused_computation.70 | loop fusion | flops 94371840 | bytes 94371840 | tf_op jit(solution)/shard_map/concatenate | solution.py:178
  1198.4 88.9 %copy.120 = bf16[10,1536,1536]{2,0,1:T(8,128)(2,1)} copy(bf16[10,1536,1536]{1,2,0:T(8,128)(2,1)} %pad_maximum_fusion) | data formatting | bytes 94371840
  1287.4 41.8 %copy.123 = bf16[192,8,10,1536]{3,1,2,0:T(8,128)(2,1)} copy(bf16[192,8,10,1536]{3,2,1,0:T(8,128)(2,1)} %bitcast.78) | data formatting | bytes 94371840
  1330.9 17.6 fusion.63
  1357.9 45.3 %all-to-all-done.3 = bf16[4,10,32,1536]{3,2,1,0:T(8,128)(2,1)} async-done(((bf16[4,10,32,1536]{3,2,1,0:T(8,128)(2,1)}), bf16[4,10,32,1536]{3,2,1,0:T(8,128)(2,1)}, u32[]{:S(2)}, u32[]{:S(2)}) %all-to-all-start.3) | async-done | bytes 3932192 | tf_op jit(solution)/shard_map/all_to_all | solution.py:290
  1426.7 38.7 %while.29 = (s32[]{:T(128)}, f32[8,3,128,64]{2,3,1,0:T(8,128)S(1)}, f32[8,128,64]{1,2,0:T(8,128)S(1)}, bf16[8,128,64]{1,2,0:T(8,128)(2,1)S(1)}, bf16[8,3,128,64]...) while((s32[]{:T(128)}, f32[8,3,128,64]{2,3,1,0:T(8,128)S(1)}, ...), condition=%wide.region_20.21_spmd.clone, body=%wide.region_18.20_spmd.clone.sunk | while | flops 31981184 | bytes 1439365 | solution.py:317
  1479.9 42.6 %all-reduce.6 = (f32[1536]{0:T(1024)S(1)}, f32[1536]{0:T(1024)S(1)}) all-reduce(f32[1536]{0:T(1024)S(1)} %get-tuple-element.196, f32[1536]{0:T(1024)S(1)} %get-tuple-element.194), channel_id=2, replica_groups=mesh['dp'=4,'fsdp'=8] {'dp','fsdp'}, use_global_device_ids=true, to_apply=%region_23.24.clone | all-reduce | flops 3072 | bytes 24576
  1526.2 544.1 %reduce-scatter.15.cloned.1.call-done = bf16[192,15360]{1,0:T(8,128)(2,1)} async-done(((bf16[1536,15360]{1,0:T(8,128)(2,1)}), bf16[192,15360]{1,0:T(8,128)(2,1)}) %reduce-scatter.15.cloned.1.call-update) | async-done | bytes 5898256
  2070.3 11.1 reshape.367
  2081.4 12.8 copy.121
  2094.2 11.2 copy.114
  2105.4 106.6 %reduce-scatter.11.cloned.1.call-done = f32[48,1536]{1,0:T(8,128)} async-done(((f32[1536,1536]{1,0:T(8,128)}), f32[48,1536]{1,0:T(8,128)}) %reduce-scatter.11.cloned.1.call-update) | async-done | bytes 294928 | tf_op jit(solution)/shard_map/reduce_scatter | solution.py:338
  2212.0 176.3 %reduce-scatter.9.cloned.1.call-done = f32[48,2560]{1,0:T(8,128)} async-done(((f32[1536,2560]{1,0:T(8,128)}), f32[48,2560]{1,0:T(8,128)}) %reduce-scatter.9.cloned.1.call-update) | async-done | bytes 491536 | tf_op jit(solution)/shard_map/reduce_scatter | solution.py:337
  (297 shorter events, 199.3 us)
Async XLA Ops:
  7.2 82.0 %all-gather.5.cloned.1.call-start = ((), (), s32[]{:S(2)}) async-start(), calls=%async_computation.8 | async-start | bytes 8110080 | tf_op jit(solution)/shard_map/all_gather | solution.py:184
  7.9 146.4 %all-gather.7.cloned.1.call-start = ((), (), s32[]{:S(2)}) async-start(), calls=%async_computation.9 | async-start | bytes 4866048 | tf_op jit(solution)/shard_map/all_gather | solution.py:185
  8.7 61.5 %copy-start = (bf16[128,1536]{1,0:T(8,128)(2,1)S(1)}, bf16[128,1536]{1,0:T(8,128)(2,1)}, u32[]{:S(2)}) copy-start(bf16[128,1536]{1,0:T(8,128)(2,1)} %param.14) | copy-start | bytes 1179652
  8.7 1045.6 %all-gather.9.cloned.1.call-start = ((), (), s32[]{:S(2)}) async-start(), calls=%async_computation.10 | async-start | bytes 53084160 | tf_op jit(solution)/shard_map/all_gather | solution.py:192
  53.8 39.9 %copy-start.21 = (f32[1536]{0:T(1024)}, f32[1536]{0:T(1024)S(1)}, u32[]{:S(2)}) copy-start(f32[1536]{0:T(1024)S(1)} %convert_element_type.124) | copy-start | bytes 18436
  53.8 103.9 %copy-start.27 = (f32[1536]{0:T(1024)}, f32[1536]{0:T(1024)S(1)}, u32[]{:S(2)}) copy-start(f32[1536]{0:T(1024)S(1)} %convert_element_type.129) | copy-start | bytes 18436
  103.6 54.0 %copy-start.6 = (bf16[8,3,128,64]{2,3,1,0:T(8,128)(2,1)}, bf16[8,3,128,64]{2,3,1,0:T(8,128)(2,1)S(1)}, u32[]{:S(2)}) copy-start(bf16[8,3,128,64]{2,3,1,0:T(8,128)(2,1)S(1)} %get-tuple-element.410) | copy-start | bytes 1179652
  103.6 55.1 %copy-start.14 = (bf16[8,3,128,64]{2,3,1,0:T(8,128)(2,1)}, bf16[8,3,128,64]{2,3,1,0:T(8,128)(2,1)S(1)}, u32[]{:S(2)}) copy-start(bf16[8,3,128,64]{2,3,1,0:T(8,128)(2,1)S(1)} %get-tuple-element.465) | copy-start | bytes 1179652
  103.6 55.1 %copy-start.23 = (bf16[8,128,64]{1,2,0:T(8,128)(2,1)}, bf16[8,128,64]{1,2,0:T(8,128)(2,1)S(1)}, u32[]{:S(2)}) copy-start(bf16[8,128,64]{1,2,0:T(8,128)(2,1)S(1)} %get-tuple-element.466) | copy-start | bytes 393220
  103.6 55.1 %copy-start.24 = (bf16[8,128,64]{1,2,0:T(8,128)(2,1)}, bf16[8,128,64]{1,2,0:T(8,128)(2,1)S(1)}, u32[]{:S(2)}) copy-start(bf16[8,128,64]{1,2,0:T(8,128)(2,1)S(1)} %get-tuple-element.467) | copy-start | bytes 393220
  164.2 150.9 %copy-start.4 = (bf16[128,1536]{1,0:T(8,128)(2,1)S(1)}, bf16[128,1536]{1,0:T(8,128)(2,1)}, u32[]{:S(2)}) copy-start(bf16[128,1536]{1,0:T(8,128)(2,1)} %param.17) | copy-start | bytes 1179652
  164.2 170.8 %all-to-all-start = ((bf16[4,10,32,1536]{3,2,1,0:T(8,128)(2,1)}), bf16[4,10,32,1536]{3,2,1,0:T(8,128)(2,1)}, u32[]{:S(2)}, u32[]{:S(2)}) async-start(bf16[4,10,32,1536]{3,2,1,0:T(8,128)(2,1)} %bitcast.245), calls=%async_computation | async-start | bytes 7864320 | tf_op jit(solution)/shard_map/all_to_all | solution.py:255
  335.0 735.1 %all-to-all-start.2 = ((bf16[4,10,32,1536]{3,2,1,0:T(8,128)(2,1)}), bf16[4,10,32,1536]{3,2,1,0:T(8,128)(2,1)}, u32[]{:S(2)}, u32[]{:S(2)}) async-start(bf16[4,10,32,1536]{3,2,1,0:T(8,128)(2,1)} %multiply_convert_fusion), calls=%async_computation.2 | async-start | bytes 7864320 | tf_op jit(solution)/shard_map/all_to_all | solution.py:281
  341.0 807.6 %copy-start.30 = (s32[1024]{0:T(1024)}, s32[1024]{0:T(1024)S(1)}, u32[]{:S(2)}) copy-start(s32[1024]{0:T(1024)S(1)} %broadcast_clamp_fusion) | copy-start | bytes 12292
  1098.4 50.2 %all-to-all-start.1 = ((bf16[4,10,32,1536]{3,2,1,0:T(8,128)(2,1)}), bf16[4,10,32,1536]{3,2,1,0:T(8,128)(2,1)}, u32[]{:S(2)}, u32[]{:S(2)}) async-start(bf16[4,10,32,1536]{3,2,1,0:T(8,128)(2,1)} %copy.105), calls=%async_computation.1 | async-start | bytes 7864320 | tf_op jit(solution)/shard_map/all_to_all | solution.py:257
  1103.2 421.6 %reduce-scatter.13.cloned.1.call-start = ((), (), s32[]{:S(2)}) async-start(), calls=%async_computation.13 | async-start | bytes 811008
  1164.6 905.7 %reduce-scatter.15.cloned.1.call-start = ((), (), s32[]{:S(2)}) async-start(), calls=%async_computation.14 | async-start | bytes 53084160
  1352.9 50.3 %copy-start.31 = (s32[1024]{0:T(1024)S(1)}, s32[1024]{0:T(1024)}, u32[]{:S(2)}) copy-start(s32[1024]{0:T(1024)} %copy-done.30) | copy-start | bytes 12292
  1352.9 50.3 %all-to-all-start.3 = ((bf16[4,10,32,1536]{3,2,1,0:T(8,128)(2,1)}), bf16[4,10,32,1536]{3,2,1,0:T(8,128)(2,1)}, u32[]{:S(2)}, u32[]{:S(2)}) async-start(bf16[4,10,32,1536]{3,2,1,0:T(8,128)(2,1)} %copy.108), calls=%async_computation.3 | async-start | bytes 7864320 | tf_op jit(solution)/shard_map/all_to_all | solution.py:290
  1357.8 854.2 %reduce-scatter.11.cloned.1.call-start = ((), (), s32[]{:S(2)}) async-start(), calls=%async_computation.12 | async-start | bytes 9732096 | tf_op jit(solution)/shard_map/reduce_scatter | solution.py:338
  1425.6 39.8 %copy-start.18 = (f32[128,32]{0,1:T(8,128)S(1)}, f32[128,32]{0,1:T(8,128)}, u32[]{:S(2)}) copy-start(f32[128,32]{0,1:T(8,128)} %copy-done.17) | copy-start | bytes 49156
  1425.6 39.8 %copy-start.20 = (f32[128,32]{0,1:T(8,128)S(1)}, f32[128,32]{0,1:T(8,128)}, u32[]{:S(2)}) copy-start(f32[128,32]{0,1:T(8,128)} %copy-done.19) | copy-start | bytes 49156
  1425.6 962.7 %reduce-scatter.9.cloned.1.call-start = ((), (), s32[]{:S(2)}) async-start(), calls=%async_computation.11 | async-start | bytes 16220160 | tf_op jit(solution)/shard_map/reduce_scatter | solution.py:337
  1426.7 39.0 %copy-start.33 = (f32[128]{0:T(128)S(1)}, f32[128]{0:T(128)}, u32[]{:S(2)}) copy-start(f32[128]{0:T(128)} %copy-done.32) | copy-start | bytes 1540
  (28 other events, 241.3 us)
Sparse Core Ops, SparseCore 0:
  11.0 78.1 all-gather.4
  92.2 62.1 all-gather.6
  155.9 898.3 all-gather.8
  1164.7 95.2 reduce-scatter.12
  1329.3 740.9 reduce-scatter.14
  2076.6 135.3 reduce-scatter.10
  2218.6 169.6 reduce-scatter.8
where the time goes:
time: 2410 us; the launch traced here: 2400 us
  waiting for transfers between devices  1680 us (70%)
  local copies, waits for them, and re-layouts  237 us (10%)
  blocking collectives  231 us (10%)
  matrix products  151 us (6%)
  other arithmetic  63.4 us (3%)
    all_gather x1, waiting for transfers between devices, fetch_experts(): return lax.all_gather(expert_weight, 'fsdp', axis=1, tiled=True)  713 us
    unnamed x9, waiting for transfers between devices  546 us
    reduce_scatter x1, waiting for transfers between devices, on_device(): lax.psum_scatter(d_qkv, ('dp', 'fsdp'), scatter_dimension=0, tiled=True)  176 us
    unnamed x96, local copies, waits for them, and re-layouts  174 us
    all_gather x1, blocking collectives, fetch_dense(): lax.all_gather(router_weight, ('dp', 'fsdp'), axis=0, tiled=True)  145 us
    reduce_scatter x1, waiting for transfers between devices, on_device(): lax.psum_scatter(d_out, ('dp', 'fsdp'), scatter_dimension=0, tiled=True)  107 us
    unnamed x2, blocking collectives  85.8 us
    all_gather x1, waiting for transfers between devices, fetch_dense(): lax.all_gather(out_weight, ('dp', 'fsdp'), axis=0, tiled=True)  50.7 us
  transfers between devices with their start and end apart: 11, of which 8 were waited for; matrix products, arithmetic and copies ran while one was open for 17% of the time, Pallas kernels for 0%

commit v1 on v0

v1 whole, which is shorter than its diff:
```python
import functools
import math

import jax
import jax.numpy as jnp
import numpy as np
from jax import lax
from jax.experimental import pallas as pl
from jax.experimental.pallas import tpu as pltpu
from jax.sharding import PartitionSpec as P

D = 1536
H = 24
KV = 8
HD = 64
E = 40
CAP = 32
AXES = ("dp", "fsdp")


norm_eps = 1e-06


def rope_tables(seq_row, half_width):
    length = seq_row.shape[0]
    places = jnp.arange(length)
    same_seq = seq_row[:, None] == seq_row[None, :]
    earlier = places[None, :] < places[:, None]
    position = jnp.sum(jnp.where(same_seq & earlier, 1, 0), axis=1).astype(jnp.int32)
    inverse = 10000.0 ** (-jnp.arange(half_width).astype(jnp.float32) / half_width)
    angles = position.astype(jnp.float32)[:, None] * inverse[None, :]
    visible = same_seq & (places[None, :] <= places[:, None])
    return (jnp.cos(angles), jnp.sin(angles), visible)


def rotate(values, cosine, sine_table):
    half_width = values.shape[-1] // 2
    first_half = values[..., :half_width]
    second_half = values[..., half_width:]
    cos_wide = cosine[:, None, :]
    sin_wide = sine_table[:, None, :]
    return jnp.concatenate(
        [
            first_half * cos_wide - second_half * sin_wide,
            second_half * cos_wide + first_half * sin_wide,
        ],
        axis=-1,
    )


def unrotate(grad_rows, cosine, sine_table):
    half_width = grad_rows.shape[-1] // 2
    first_half = grad_rows[..., :half_width]
    second_half = grad_rows[..., half_width:]
    cos_wide = cosine[:, None, :]
    sin_wide = sine_table[:, None, :]
    return jnp.concatenate(
        [
            first_half * cos_wide + second_half * sin_wide,
            second_half * cos_wide - first_half * sin_wide,
        ],
        axis=-1,
    )


def norm_forward(values, gain_vec):
    inv_rms = lax.rsqrt(jnp.mean(values * values, axis=-1, keepdims=True) + norm_eps)
    return (inv_rms, values * inv_rms * gain_vec.astype(jnp.float32))


def norm_backward(values, inv_rms, gain_vec, upstream):
    weighted = upstream * gain_vec.astype(jnp.float32)
    d_gain = jnp.sum(upstream * values * inv_rms, axis=0)
    d_values = inv_rms * (
        weighted - values * inv_rms * inv_rms * jnp.mean(weighted * values, axis=-1, keepdims=True)
    )
    return (d_values, d_gain)


def attend_group(group_in, visible, factor):
    queries, keys_rot, values_in = group_in
    scores = (
        jnp.einsum("gqd,kd->gqk", queries, keys_rot, preferred_element_type=jnp.float32) * factor
    )
    exp_scores = jnp.where(visible[None], jnp.exp(scores), 0.0)
    totals = jnp.sum(exp_scores, axis=-1)
    attn_probs = (exp_scores / totals[..., None]).astype(jnp.bfloat16)
    mixed_heads = jnp.einsum(
        "gqk,kd->gqd", attn_probs, values_in, preferred_element_type=jnp.float32
    )
    return (mixed_heads.astype(jnp.bfloat16), jnp.log(totals))


def attend_back(group_in, visible, factor):
    queries, keys_rot, values_in, mixed_heads, log_totals, d_mixed = group_in
    scores = (
        jnp.einsum("gqd,kd->gqk", queries, keys_rot, preferred_element_type=jnp.float32) * factor
    )
    recomputed = jnp.where(visible[None], jnp.exp(scores - log_totals[..., None]), 0.0)
    row_delta = jnp.sum(d_mixed.astype(jnp.float32) * mixed_heads.astype(jnp.float32), axis=-1)
    d_probs = jnp.einsum("gqd,kd->gqk", d_mixed, values_in, preferred_element_type=jnp.float32)
    d_scores = (recomputed * (d_probs - row_delta[..., None])).astype(jnp.bfloat16)
    d_query = (
        jnp.einsum("gqk,kd->gqd", d_scores, keys_rot, preferred_element_type=jnp.float32) * factor
    )
    d_keys = (
        jnp.einsum("gqk,gqd->kd", d_scores, queries, preferred_element_type=jnp.float32) * factor
    )
    d_values = jnp.einsum(
        "gqk,gqd->kd", recomputed.astype(jnp.bfloat16), d_mixed, preferred_element_type=jnp.float32
    )
    return (d_query, d_keys, d_values)


def bit_groups():
    dp_count, fsdp_count = lax.axis_size("dp"), lax.axis_size("fsdp")
    fsdp_bits = int(math.log2(fsdp_count))
    low = fsdp_bits // 2
    near = [m for m in range(1, 1 << low)]
    far = [m << low for m in range(1, fsdp_count >> low)]
    core = fsdp_count
    rows = [m * 2 * fsdp_count for m in range(1, dp_count // 2)]
    return far, near, rows, core


def swap(value, mask):
    count = lax.axis_size("dp") * lax.axis_size("fsdp")
    return lax.ppermute(value, AXES, [(i, i ^ mask) for i in range(count)])


def mask_order():
    far, near, rows, core = bit_groups()
    z_masks = [0] + far
    plane = [0] + near + rows + [a ^ b for a in near for b in rows]
    half = [p ^ z for p in plane for z in z_masks]
    return half + [m ^ core for m in half]


def spread(block):
    far, near, rows, core = bit_groups()
    mine = jnp.stack([block] + [swap(block, m) for m in far])
    cut = mine.shape[0] // 2
    by_near = [swap(mine, m) for m in near]
    by_rows = [swap(mine, m) for m in rows]
    both = []
    for a, got_a in zip(near, by_near):
        for b, got_b in zip(rows, by_rows):
            both.append(swap(got_a[:cut], b))
            both.append(swap(got_b[cut:], a))
    first = jnp.concatenate([mine] + by_near + by_rows + both)
    cut = first.shape[0] // 2
    first, second = first[:cut], first[cut:]
    return [first, second, swap(first, core), swap(second, core)]


def gather_sum(keep, send):
    far, near, rows, core = bit_groups()
    n_far, n_near, n_rows = len(far) + 1, len(near), len(rows)
    wide = jnp.float32
    cut = n_far // 2

    def add(*terms):
        return functools.reduce(jnp.add, [t.astype(wide) for t in terms]).astype(keep.dtype)

    got = swap(send, core)

    def own(i, low=0, high=n_far):
        at = slice(i * n_far + low, i * n_far + high)
        return add(keep[at], got[at])

    base = 1 + n_near + n_rows
    near_low = [own(1 + i, 0, cut) for i in range(n_near)]
    near_high = [[own(1 + i, cut)] for i in range(n_near)]
    rows_low = [[own(1 + n_near + j, 0, cut)] for j in range(n_rows)]
    rows_high = [own(1 + n_near + j, cut) for j in range(n_rows)]
    for i, a in enumerate(near):
        for j, b in enumerate(rows):
            at = base + i * n_rows + j
            rows_low[j].append(swap(own(at, 0, cut), a))
            near_high[i].append(swap(own(at, cut), b))
    low, high = [own(0, 0, cut)], [own(0, cut)]
    for i, a in enumerate(near):
        low.append(swap(near_low[i], a))
        high.append(swap(add(*near_high[i]), a))
    for j, b in enumerate(rows):
        low.append(swap(add(*rows_low[j]), b))
        high.append(swap(rows_high[j], b))
    mine = [add(*[t[i] for t in low]) for i in range(cut)]
    mine += [add(*[t[i] for t in high]) for i in range(n_far - cut)]
    total = mine[0].astype(wide)
    for m, piece in zip(far, mine[1:]):
        total = total + swap(piece, m).astype(wide)
    return total


def take_blocks_kernel(order_ref, *refs):
    column = 0
    for ref in refs[:-1]:
        width = ref.shape[-1]
        refs[-1][0, :, column : column + width] = ref[0].astype(refs[-1].dtype)
        column += width


def take_blocks(arrays, order):
    count = order.shape[0]
    blocks = [a.reshape((count, a.shape[0] // count, a.shape[1])) for a in arrays]
    rows, width = blocks[0].shape[1], sum(a.shape[1] for a in arrays)
    return pl.pallas_call(
        take_blocks_kernel,
        out_shape=jax.ShapeDtypeStruct((count, rows, width), jnp.bfloat16),
        grid_spec=pltpu.PrefetchScalarGridSpec(
            num_scalar_prefetch=1,
            grid=(count,),
            in_specs=[
                pl.BlockSpec((1, rows, a.shape[2]), lambda g, order: (order[g], 0, 0)) for a in blocks
            ],
            out_specs=pl.BlockSpec((1, rows, width), lambda g, order: (g, 0, 0)),
        ),
        name="take_blocks",
    )(order, *blocks)


def pack_kernel(fs, w_ref, u_ref):
    slices = u_ref.shape[0]
    for s in range(slices):
        for p in range(3):
            u_ref[s, :, p * fs : (p + 1) * fs] = w_ref[0, :, (p * slices + s) * fs : (p * slices + s + 1) * fs]


def pack_units(weight, slices):
    local, dl, cols = weight.shape
    fs = cols // 3 // slices
    return pl.pallas_call(
        functools.partial(pack_kernel, fs),
        out_shape=jax.ShapeDtypeStruct((local * slices, dl, 3 * fs), weight.dtype),
        grid=(local,),
        in_specs=[pl.BlockSpec((1, dl, cols), lambda g: (g, 0, 0))],
        out_specs=pl.BlockSpec((slices, dl, 3 * fs), lambda g: (g, 0, 0)),
        name="pack_units",
    )(weight)


def unpack_kernel(fs, u_ref, w_ref):
    slices = u_ref.shape[0]
    for s in range(slices):
        for p in range(3):
            w_ref[0, :, (p * slices + s) * fs : (p * slices + s + 1) * fs] = u_ref[
                s, :, p * fs : (p + 1) * fs
            ].astype(w_ref.dtype)


def unpack_units(units, slices):
    count, dl, width = units.shape
    fs, local = width // 3, count // slices
    return pl.pallas_call(
        functools.partial(unpack_kernel, fs),
        out_shape=jax.ShapeDtypeStruct((local, dl, width * slices), jnp.float32),
        grid=(local,),
        in_specs=[pl.BlockSpec((slices, dl, width), lambda g: (g, 0, 0))],
        out_specs=pl.BlockSpec((1, dl, width * slices), lambda g: (g, 0, 0)),
        name="unpack_units",
    )(units)


def unit_plan(local_count, fsdp_count):
    slices = fsdp_count // math.gcd(local_count, fsdp_count)
    per = local_count * slices // fsdp_count
    table = []
    for place in range(fsdp_count):
        owners = [(per * place + i) // slices for i in range(per)]
        second = owners[-1] if owners[-1] != owners[0] else -1
        table.append([owners[0], second] + [o - owners[0] for o in owners])
    return slices, per, np.array(table, np.int32)


def moe_kernel(per, sel_ref, x0, x1, x2, x3, c0, c1, c2, c3, routes_ref, router_ref, w_ref,
               y_keep, y_send, dx_keep, dx_send, dg_ref, dw_ref,
               x_buf, c_buf, rows_x, rows_c, dboth_s, gh_s, hot_s, gate_s, y_acc, dx_acc, dgs_s, sems, *dw_acc):
    step = pl.program_id(0)
    steps = 4 * x0.shape[0] // x_buf.shape[1]
    _, sb, length, width = x_buf.shape
    each = steps // 4

    def fetch(k):
        at = pl.ds((k % each) * sb, sb)
        for n, (pieces, buf) in enumerate((((x0, x1, x2, x3), x_buf), ((c0, c1, c2, c3), c_buf))):
            pltpu.make_async_copy(pieces[k // each].at[at], buf.at[k % 2], sems.at[n, k % 2]).start()

    @pl.when(step == 0)
    def _():
        fetch(0)

    for k in range(1, steps):

        @pl.when(step == k - 1)
        def _():
            fetch(k)

    slot = lax.rem(step, 2)
    for n, buf in enumerate((x_buf, c_buf)):
        pltpu.make_async_copy(x0.at[pl.ds(0, sb)], buf.at[slot], sems.at[n, slot]).wait()
    x_ref, cot_ref = x_buf.at[slot], c_buf.at[slot]
    fs = w_ref.shape[-1] // 3
    rows = sb * CAP
    f32, bf16 = jnp.float32, jnp.bfloat16
    experts = router_ref.shape[0]
    first, second = sel_ref[0], sel_ref[1]
    round_steps = rows_x.shape[1] // rows
    base = lax.rem(step, round_steps) * rows
    lane = lax.broadcasted_iota(jnp.int32, (length, length), 1)
    sub = lax.broadcasted_iota(jnp.int32, (length, length), 0)
    before = jnp.where(sub < lane, 1.0, 0.0).astype(bf16)
    slot_iota = lax.broadcasted_iota(jnp.int32, (CAP, length), 0)
    expert_iota = lax.broadcasted_iota(jnp.int32, (experts, length), 0)
    masks = []
    for s in range(sb):
        r = routes_ref[s]
        for e in (first, second):
            masks.append(jnp.sum(jnp.where(r == e, 1.0, 0.0), axis=0, keepdims=True))
    mask_all = jnp.concatenate(masks, axis=0)
    slot_all = jnp.dot(mask_all.astype(bf16), before, preferred_element_type=f32).astype(jnp.int32)
    for s in range(sb):
        r = routes_ref[s]
        x = x_ref[s]
        c = cot_ref[s]
        logits = lax.dot_general(router_ref[...], x, (((1,), (1,)), ((), ())), preferred_element_type=f32)
        chosen = jnp.zeros((experts, length), f32)
        for j in range(r.shape[0]):
            chosen = chosen + jnp.where(r[j : j + 1, :] == expert_iota, 1.0, 0.0)
        expo = jnp.where(chosen > 0.0, jnp.exp(logits), 0.0)
        gates = expo / jnp.sum(expo, axis=0, keepdims=True)
        hots = []
        for k, e in enumerate((first, second)):
            row = 2 * s + k
            hot = jnp.where(
                (slot_iota == slot_all[row : row + 1, :]) & (mask_all[row : row + 1, :] > 0.0), 1.0, 0.0
            )
            grow = jnp.sum(jnp.where(expert_iota == e, gates, 0.0), axis=0, keepdims=True)
            gate_s[k, pl.ds(s * CAP, CAP), :] = jnp.sum(hot * grow, axis=1, keepdims=True)
            hots.append(hot)
        hot2 = jnp.concatenate(hots, axis=0).astype(bf16)
        hot_s[s] = hot2
        got_x = jnp.dot(hot2, x, preferred_element_type=f32).astype(bf16)
        got_c = jnp.dot(hot2, c, preferred_element_type=f32).astype(bf16)
        for k in range(2):
            at = pl.ds(pl.multiple_of(base + s * CAP, CAP), CAP)
            rows_x[k, at, :] = got_x[k * CAP : (k + 1) * CAP]
            rows_c[k, at, :] = got_c[k * CAP : (k + 1) * CAP]
    y_acc[...] = jnp.zeros_like(y_acc)
    dx_acc[...] = jnp.zeros_like(dx_acc)
    dgs_s[...] = jnp.zeros_like(dgs_s)
    here = pl.ds(pl.multiple_of(base, rows), rows)
    for i in range(per):
        k = sel_ref[2 + i]
        w = w_ref[:, i].reshape(width, 3 * fs)
        w_gu, w_d = w[:, : 2 * fs], w[:, 2 * fs :]
        both = jnp.dot(rows_x[k, here, :], w_gu, preferred_element_type=f32)
        gate, up = both[:, :fs], both[:, fs:]
        sig = jax.nn.sigmoid(gate)
        hidden = (gate * sig * up).astype(bf16).astype(f32)
        dh_raw = jnp.dot(rows_c[k, here, :], w_d, preferred_element_type=f32)
        g = gate_s[k]
        dgs_s[k] += jnp.sum(hidden * dh_raw, axis=1, keepdims=True)
        dh = g * dh_raw
        dboth = jnp.concatenate(
            [dh * up * sig * (1.0 + gate * (1.0 - sig)), dh * gate * sig], axis=1
        ).astype(bf16)
        gh = (g * hidden).astype(bf16)
        dboth_s[i, here, :] = dboth
        gh_s[i, here, :] = gh
        contract = (((1,), (1,)), ((), ()))
        y_acc[k] += lax.dot_general(gh, w_d, contract, preferred_element_type=f32)
        dx_acc[k] += lax.dot_general(dboth, w_gu, contract, preferred_element_type=f32)
    contract = (((0,), (0,)), ((), ()))
    for s in range(sb):
        at = pl.ds(s * CAP, CAP)
        hot2 = hot_s[s]
        y2 = jnp.concatenate([y_acc[0, at, :], y_acc[1, at, :]], axis=0).astype(bf16)
        y = lax.dot_general(hot2, y2, contract, preferred_element_type=f32).astype(bf16)
        d2 = jnp.concatenate([dx_acc[0, at, :], dx_acc[1, at, :]], axis=0).astype(bf16)
        d = lax.dot_general(hot2, d2, contract, preferred_element_type=f32).astype(bf16)

        @pl.when(step < steps // 2)
        def _():
            y_keep[s] = y
            dx_keep[s] = d

        @pl.when(step >= steps // 2)
        def _():
            y_send[s] = y
            dx_send[s] = d

        hot = hot2.astype(f32)
        for k in range(2):
            dg_ref[s, k : k + 1, :] = jnp.sum(
                hot[k * CAP : (k + 1) * CAP] * dgs_s[k, at, :], axis=0, keepdims=True
            )

    @pl.when(lax.rem(step, round_steps) == round_steps - 1)
    def _():
        places, _, dl, _ = dw_ref.shape
        for i in range(per):
            k = sel_ref[2 + i]
            gu = lax.dot_general(rows_x[k], dboth_s[i], contract, preferred_element_type=f32)
            dd = lax.dot_general(rows_c[k], gh_s[i], contract, preferred_element_type=f32)
            if dw_acc:
                gu = gu + jnp.where(step < round_steps, 0.0, dw_acc[0][i, :, : 2 * fs])
                dd = dd + jnp.where(step < round_steps, 0.0, dw_acc[0][i, :, 2 * fs :])
                dw_acc[0][i, :, : 2 * fs] = gu
                dw_acc[0][i, :, 2 * fs :] = dd
            dw_ref[:, i, :, : 2 * fs] = gu.astype(bf16).reshape(places, dl, 2 * fs)
            dw_ref[:, i, :, 2 * fs :] = dd.astype(bf16).reshape(places, dl, fs)


def moe(sel, x_pieces, cot_pieces, routes_all, router_t, units):
    quarter, length, width = x_pieces[0].shape
    count = 4 * quarter
    places, per, dl, cols = units.shape
    fs = cols // 3
    sb = 4
    steps = count // sb
    half = steps // 2
    bf16, f32 = jnp.bfloat16, jnp.float32
    rounds = max(1, count // 32)
    slots = count * CAP // rounds
    keep = pl.BlockSpec((sb, length, width), lambda g, sel: (jnp.minimum(g, half - 1), 0, 0))
    send = pl.BlockSpec((sb, length, width), lambda g, sel: (jnp.maximum(g - half, 0), 0, 0))
    part = jax.ShapeDtypeStruct((2 * quarter, length, width), bf16)
    whole4 = lambda g, sel: (0, 0, 0, 0)
    return pl.pallas_call(
        functools.partial(moe_kernel, per),
        out_shape=(
            part,
            part,
            part,
            part,
            jax.ShapeDtypeStruct((count, 2, length), f32),
            jax.ShapeDtypeStruct(units.shape, bf16),
        ),
        grid_spec=pltpu.PrefetchScalarGridSpec(
            num_scalar_prefetch=1,
            grid=(steps,),
            in_specs=[pl.BlockSpec(memory_space=pl.ANY)] * 8
            + [
                pl.BlockSpec((sb,) + routes_all.shape[1:], lambda g, sel: (g, 0, 0)),
                pl.BlockSpec(router_t.shape, lambda g, sel: (0, 0), pipeline_mode=pl.Buffered(1)),
                pl.BlockSpec(units.shape, whole4, pipeline_mode=pl.Buffered(1)),
            ],
            out_specs=[
                keep,
                send,
                keep,
                send,
                pl.BlockSpec((sb, 2, length), lambda g, sel: (g, 0, 0)),
                pl.BlockSpec(units.shape, whole4, pipeline_mode=pl.Buffered(1)),
            ],
            scratch_shapes=[
                pltpu.VMEM((2, sb, length, width), bf16),
                pltpu.VMEM((2, sb, length, width), bf16),
                pltpu.VMEM((2, slots, width), bf16),
                pltpu.VMEM((2, slots, width), bf16),
                pltpu.VMEM((per, slots, 2 * fs), bf16),
                pltpu.VMEM((per, slots, fs), bf16),
                pltpu.VMEM((sb, 2 * CAP, length), bf16),
                pltpu.VMEM((2, sb * CAP, 1), f32),
                pltpu.VMEM((2, sb * CAP, width), f32),
                pltpu.VMEM((2, sb * CAP, width), f32),
                pltpu.VMEM((2, sb * CAP, 1), f32),
                pltpu.SemaphoreType.DMA((2, 2)),
            ]
            + [pltpu.VMEM((per, width, cols), f32)] * (rounds > 1),
        ),
        compiler_params=pltpu.CompilerParams(
            dimension_semantics=("arbitrary",), vmem_limit_bytes=60 << 20
        ),
        cost_estimate=pl.CostEstimate(
            flops=2 * count * CAP * per * fs * width * 9,
            transcendentals=count * CAP * per * fs,
            bytes_accessed=4 * count * length * width * 2,
        ),
        name="moe",
    )(sel, *x_pieces, *cot_pieces, routes_all, router_t, units)


def on_device(
    tokens,
    seq_ids,
    routes,
    cotangent,
    gain_attn,
    qkv_weight,
    out_weight,
    gain_moe,
    router_weight,
    expert_weight,
):
    length = tokens.shape[0]
    fsdp_count = lax.axis_size("fsdp")
    dp_count = lax.axis_size("dp")
    count = dp_count * fsdp_count
    local_count, dl, cols = expert_weight.shape
    hidden_width = cols // 3
    slices, per, table = unit_plan(local_count, fsdp_count)
    fs = hidden_width // slices
    query_width = H * HD
    kv_width = KV * HD
    group_size = H // KV
    factor = HD ** (-0.5)
    bf16, f32 = jnp.bfloat16, jnp.float32
    dp_at, fsdp_at = lax.axis_index("dp"), lax.axis_index("fsdp")
    me = dp_at * fsdp_count + fsdp_at
    order = jnp.asarray(np.array(mask_order(), np.int32)) ^ me

    own_rows = qkv_weight.shape[0]
    route_cols = -(-routes.size // own_rows)
    coded = jnp.zeros((own_rows * route_cols,), bf16).at[: routes.size].set(routes.T.reshape(-1).astype(bf16))
    coded = coded.reshape(own_rows, route_cols)
    pad = jnp.zeros((own_rows, 128 - E - 2 - route_cols), bf16)
    small = jnp.concatenate(
        [qkv_weight, router_weight, gain_attn[:, None], gain_moe[:, None], coded, pad], axis=1
    )
    qkv_small = lax.all_gather(small, AXES, axis=0, tiled=True)
    out_full = lax.all_gather(out_weight, AXES, axis=0, tiled=True)
    qkv_full = qkv_small[:, : qkv_weight.shape[1]]
    tail = qkv_small[:, qkv_weight.shape[1] :]
    router_full, gain_one, gain_two = tail[:, :E], tail[:, E], tail[:, E + 1]
    routes_all = tail.reshape(count, own_rows, 128)[:, :, E + 2 : E + 2 + route_cols].reshape(count, -1)
    routes_all = routes_all[:, : routes.size].reshape(count, routes.shape[1], length).astype(jnp.int32)
    routes_all = routes_all[order]

    units = pack_units(expert_weight, slices).reshape(fsdp_count, per, dl, 3 * fs)
    units = lax.all_to_all(units, "fsdp", split_axis=0, concat_axis=0, tiled=True)
    cot_all = spread(cotangent)
    sel = jnp.asarray(table)[fsdp_at]
    shift = jnp.where(sel[:2] >= 0, dp_at * local_count, 0)
    sel = jnp.concatenate([sel[:2] + shift, sel[2:]])

    cosine, sine_table, visible = rope_tables(seq_ids[0], HD // 2)
    stream_in = tokens.astype(f32)
    inv_one, normed = norm_forward(stream_in, gain_one)
    normed_one = normed.astype(bf16)
    qkv_proj = jnp.dot(normed_one, qkv_full, preferred_element_type=f32)
    queries = rotate(qkv_proj[:, :query_width].reshape(length, H, HD), cosine, sine_table).astype(bf16)
    keys_rot = rotate(
        qkv_proj[:, query_width : query_width + kv_width].reshape(length, KV, HD), cosine, sine_table
    ).astype(bf16)
    values_in = qkv_proj[:, query_width + kv_width :].reshape(length, KV, HD).astype(bf16)
    query_groups = queries.reshape(length, KV, group_size, HD).transpose(1, 2, 0, 3)
    key_groups = keys_rot.transpose(1, 0, 2)
    value_groups = values_in.transpose(1, 0, 2)

    def forward_group(group_in):
        return attend_group(group_in, visible, factor)

    mixed_groups, log_totals = lax.map(forward_group, (query_groups, key_groups, value_groups))
    mixed_flat = mixed_groups.transpose(2, 0, 1, 3).reshape(length, query_width)
    resid_mid = stream_in + jnp.dot(mixed_flat, out_full, preferred_element_type=f32)
    inv_two, normed = norm_forward(resid_mid, gain_two)
    normed_two = normed.astype(bf16)

    x_all = spread(normed_two)
    y_keep, y_send, dx_keep, dx_send, dg_parts, dw_units = moe(sel, x_all, cot_all, routes_all, router_full.T, units)

    logits = jnp.dot(normed_two, router_full, preferred_element_type=f32)
    chosen = jnp.any(routes[:, :, None] == jnp.arange(E)[None, None, :], axis=1)
    expo = jnp.where(chosen, jnp.exp(logits), 0.0)
    gates = expo / jnp.sum(expo, axis=-1, keepdims=True)
    inverse = jnp.asarray(np.argsort(np.array(mask_order())).astype(np.int32))
    dg_natural = dg_parts[inverse[jnp.arange(count) ^ me]]
    dg_got = lax.all_to_all(dg_natural, AXES, split_axis=0, concat_axis=0, tiled=True)
    owner = np.zeros((E, count, 2), np.float32)
    for device in range(count):
        for k in range(2):
            local = table[device % fsdp_count, k]
            if local >= 0:
                owner[(device // fsdp_count) * local_count + local, device, k] = 1.0
    d_gates = jnp.einsum("edk,dkt->te", jnp.asarray(owner), dg_got, precision=lax.Precision.HIGHEST)
    d_gates = jnp.where(chosen, d_gates, 0.0)
    d_logits = (gates * (d_gates - jnp.sum(gates * d_gates, axis=-1, keepdims=True))).astype(bf16)

    d_normed_two = gather_sum(dx_keep, dx_send) + jnp.dot(d_logits, router_full.T, preferred_element_type=f32)
    d_block = cotangent.astype(f32)
    d_router = jnp.dot(normed_two.T, d_logits, preferred_element_type=f32)
    d_resid, d_gain_two = norm_backward(resid_mid, inv_two, gain_two, d_normed_two)
    d_resid = d_resid + d_block
    d_resid_half = d_resid.astype(bf16)
    d_out = jnp.dot(mixed_flat.T, d_resid_half, preferred_element_type=f32)
    d_mixed = jnp.dot(d_resid_half, out_full.T, preferred_element_type=f32).astype(bf16)
    d_mixed_groups = d_mixed.reshape(length, KV, group_size, HD).transpose(1, 2, 0, 3)

    def backward_group(group_in):
        return attend_back(group_in, visible, factor)

    d_query, d_keys, d_values = lax.map(
        backward_group,
        (query_groups, key_groups, value_groups, mixed_groups, log_totals, d_mixed_groups),
    )
    d_query = unrotate(d_query.transpose(2, 0, 1, 3).reshape(length, H, HD), cosine, sine_table)
    d_keys = unrotate(d_keys.transpose(1, 0, 2), cosine, sine_table)
    d_qkv_act = jnp.concatenate(
        [
            d_query.reshape(length, query_width),
            d_keys.reshape(length, kv_width),
            d_values.transpose(1, 0, 2).reshape(length, kv_width),
        ],
        axis=-1,
    ).astype(bf16)
    d_qkv = jnp.dot(normed_one.T, d_qkv_act, preferred_element_type=f32)
    d_normed_one = jnp.dot(d_qkv_act, qkv_full.T, preferred_element_type=f32)
    d_stream, d_gain_one = norm_backward(stream_in, inv_one, gain_one, d_normed_one)
    d_tokens = d_stream + d_resid

    block_out = (resid_mid + gather_sum(y_keep, y_send)).astype(bf16)
    d_out = take_blocks([d_out], order)
    d_out_weight = gather_sum(d_out[: count // 2], d_out[count // 2 :])
    thin = jnp.concatenate(
        [d_router, d_gain_one[:, None], d_gain_two[:, None], jnp.zeros((D, 128 - E - 2), f32)], axis=1
    )
    d_qkv = take_blocks([d_qkv, thin], order)
    d_qkv = gather_sum(d_qkv[: count // 2], d_qkv[count // 2 :])
    d_qkv_weight, thin = d_qkv[:, : qkv_weight.shape[1]], d_qkv[:, qkv_weight.shape[1] :]
    dw = lax.all_to_all(dw_units, "fsdp", split_axis=0, concat_axis=0, tiled=True)
    d_expert_weight = unpack_units(dw.reshape(local_count * slices, dl, 3 * fs), slices)
    return (
        block_out,
        d_tokens,
        thin[:, E],
        d_qkv_weight,
        d_out_weight,
        thin[:, E + 1],
        thin[:, :E],
        d_expert_weight,
    )


def solution(mesh):
    rows = P(AXES, None)
    in_specs = (rows, rows, rows, rows, P(AXES), rows, rows, P(AXES), rows, P("dp", "fsdp", None))
    out_specs = (rows, rows, P(AXES), rows, rows, P(AXES), rows, P("dp", "fsdp", None))
    return jax.shard_map(
        on_device, mesh=mesh, in_specs=in_specs, out_specs=out_specs, check_vma=False
    )
```

time: 2410 us -> 952 us (0.40)
  waiting for transfers between devices: 1680 us -> 499 us
  blocking collectives: 231 us -> 0 us
  local copies, waits for them, and re-layouts: 237 us -> 55.7 us
  Pallas kernels: 0 us -> 132 us
  starting transfers between devices: 20.9 us -> 117 us
  matrix products: 151 us -> 77.1 us
    all_gather x3 -> x2, waiting for transfers between devices: 783 us -> 197 us  [the longest x1 151 us: on_device(): qkv_small = lax.all_gather(small, AXES, axis=0, tiled=True)]
    unnamed x9 -> x2, waiting for transfers between devices: 546 us -> 0.71 us
    ppermute x0 -> x58, waiting for transfers between devices: none -> 295 us  [swap(): return lax.ppermute(value, AXES, [(i, i ^ mask) for i in range(count)])]
    reduce_scatter x2 -> x0, waiting for transfers between devices: 283 us -> none  [the longest x1 176 us: on_device(): lax.psum_scatter(d_qkv, ('dp', 'fsdp'), scatter_dimension=0, tiled=True)]
    unnamed x96 -> x85, local copies, waits for them, and re-layouts: 174 us -> 15.1 us
    all_gather x1 -> x0, blocking collectives: 145 us -> none  [fetch_dense(): lax.all_gather(router_weight, ('dp', 'fsdp'), axis=0, tiled=True)]
    pallas_call x0 -> x5, Pallas kernels: none -> 132 us  [the longest x1 72.5 us: moe(): pl.pallas_call(functools.partial(moe_kernel, per), out_shape=(part, part,...]
    ppermute x0 -> x58, starting transfers between devices: none -> 91.4 us  [swap(): return lax.ppermute(value, AXES, [(i, i ^ mask) for i in range(count)])]
  transfers between devices with their start and end apart: 11 -> 63, of which waited for: 8 -> 26; matrix products, arithmetic and copies ran while one was open for 17% -> 18% of each run, Pallas kernels for 0% -> 6%
where the time goes in v1:
time: 952 us; the launch traced here: 941 us
  waiting for transfers between devices  499 us (52%)
  Pallas kernels  132 us (14%)
  starting transfers between devices  117 us (12%)
  matrix products  77.1 us (8%)
  local copies, waits for them, and re-layouts  55.7 us (6%)
  other arithmetic  44.7 us (5%)
  between operations  14.9 us (2%)
    ppermute x58, waiting for transfers between devices, swap(): return lax.ppermute(value, AXES, [(i, i ^ mask) for i in range(count)])  295 us
    all_gather x1, waiting for transfers between devices, on_device(): qkv_small = lax.all_gather(small, AXES, axis=0, tiled=True)  151 us
    ppermute x58, starting transfers between devices, swap(): return lax.ppermute(value, AXES, [(i, i ^ mask) for i in range(count)])  91.4 us
    pallas_call x1, Pallas kernels, moe(): pl.pallas_call(functools.partial(moe_kernel, per), out_shape=(part, part,...  72.5 us
    all_gather x1, waiting for transfers between devices, on_device(): out_full = lax.all_gather(out_weight, AXES, axis=0, tiled=True)  46.5 us
    pallas_call x2, Pallas kernels, take_blocks(): pl.pallas_call(take_blocks_kernel, out_shape=jax.ShapeDtypeStruct((count,...  40.6 us
    convert_element_type x16, other arithmetic, add(): functools.reduce(jnp.add, [t.astype(wide) for t in terms])  24.4 us
  transfers between devices with their start and end apart: 63, of which 26 were waited for; matrix products, arithmetic and copies ran while one was open for 18% of the time, Pallas kernels for 6%

profile of v1, /device:TPU:0, one launch (start us, length us, event | category | flops | bytes accessed | tf_op | source)
XLA Modules:
  0.0 940.7 jit_solution(13195183883588271577)
XLA Ops:
  36.7 12.4 %collective-permute-done.10 = bf16[128,1536]{1,0:T(8,128)(2,1)S(1)} collective-permute-done((bf16[128,1536]{1,0:T(8,128)(2,1)}, bf16[128,1536]{1,0:T(8,128)(2,1)S(1)}, u32[]{:S(2)}, u32[]{:S(2)}) %collective-permute-start.10) | collective-permute-done | bytes 393248 | tf_op jit(solution)/shard_map/ppermute | solution.py:128
  52.0 17.3 %collective-permute-start.12 = (bf16[4,128,1536]{2,1,0:T(8,128)(2,1)}, bf16[4,128,1536]{2,1,0:T(8,128)(2,1)}, u32[]{:S(2)}, u32[]{:S(2)}) collective-permute-start(bf16[4,128,1536]{2,1,0:T(8,128)(2,1)} %pad_maximum_fusion.1), channel_id=1, source_target_pairs={{0,1},{1,0},{2,3},{3,2},{4,5},{5,4},{6,7},{7,6},{8,9},{9,8},{10,11... | collective-permute-start | bytes 4718600 | tf_op jit(solution)/shard_map/ppermute | solution.py:128
  70.9 150.9 %all-gather.3.cloned.1.call-done = bf16[1536,2688]{1,0:T(8,128)(2,1)} async-done(((bf16[48,2688]{1,0:T(8,128)(2,1)}), bf16[1536,2688]{1,0:T(8,128)(2,1)}) %all-gather.3.cloned.1.call-update) | async-done | bytes 8257552 | tf_op jit(solution)/shard_map/all_gather | solution.py:522
  232.0 9.0 while.29
  240.9 46.5 %all-gather.5.cloned.1.call-done = bf16[1536,1536]{1,0:T(8,128)(2,1)} async-done(((bf16[48,1536]{1,0:T(8,128)(2,1)}), bf16[1536,1536]{1,0:T(8,128)(2,1)}) %all-gather.5.cloned.1.call-update) | async-done | bytes 4718608 | tf_op jit(solution)/shard_map/all_gather | solution.py:523
  310.4 12.4 %collective-permute-done.1 = bf16[128,1536]{1,0:T(8,128)(2,1)S(1)} collective-permute-done((bf16[128,1536]{1,0:T(8,128)(2,1)S(1)}, bf16[128,1536]{1,0:T(8,128)(2,1)S(1)}, u32[]{:S(2)}, u32[]{:S(2)}) %collective-permute-start.1) | collective-permute-done | bytes 393248 | tf_op jit(solution)/shard_map/ppermute | solution.py:128
  331.2 25.6 %collective-permute-done.3 = bf16[4,128,1536]{2,1,0:T(8,128)(2,1)S(1)} collective-permute-done((bf16[4,128,1536]{2,1,0:T(8,128)(2,1)S(1)}, bf16[4,128,1536]{2,1,0:T(8,128)(2,1)S(1)}, u32[]{:S(2)}, u32[]{:S(2)}) %collective-permute-start.3) | collective-permute-done | bytes 1572896 | tf_op jit(solution)/shard_map/ppermute | solution.py:128
  368.6 9.8 %collective-permute-done.5 = bf16[2,128,1536]{2,1,0:T(8,128)(2,1)S(1)} collective-permute-done((bf16[2,128,1536]{2,1,0:T(8,128)(2,1)S(1)}, bf16[2,128,1536]{2,1,0:T(8,128)(2,1)S(1)}, u32[]{:S(2)}, u32[]{:S(2)}) %collective-permute-start.5) | collective-permute-done | bytes 786464 | tf_op jit(solution)/shard_map/ppermute | solution.py:128
  386.4 72.5 %moe.1 = (bf16[16,128,1536]{2,1,0:T(8,128)(2,1)}, bf16[16,128,1536]{2,1,0:T(8,128)(2,1)}, bf16[16,128,1536]{2,1,0:T(8,128)(2,1)}, bf16[16,128,1536]{2,1,0:T(8,12...) custom-call(s32[7]{0:T(128)} %pad_add_fusion.sel_ref, ...), custom_call_target="tpu_custom_call" | custom-call | flops 18119393280 | bytes 50331648 | tf_op jit(solution)/shard_map/moe/pallas_call | solution.py:430
  462.9 11.2 %all-to-all-start.1 = ((f32[32,2,128]{2,1,0:T(2,128)}), f32[32,2,128]{2,1,0:T(2,128)S(1)}, u32[]{:S(2)}, u32[]{:S(2)}) async-start(f32[32,2,128]{2,1,0:T(2,128)} %gather_fusion.2), calls=%async_computation.1 | async-start | bytes 65536 | tf_op jit(solution)/shard_map/all_to_all | solution.py:570
  481.3 8.6 all-to-all-start.2
  504.1 54.2 %collective-permute-done.20 = bf16[2,128,1536]{2,1,0:T(8,128)(2,1)S(1)} collective-permute-done((bf16[2,128,1536]{2,1,0:T(8,128)(2,1)S(1)}, bf16[2,128,1536]{2,1,0:T(8,128)(2,1)S(1)}, u32[]{:S(2)}, u32[]{:S(2)}) %collective-permute-start.20) | collective-permute-done | bytes 786464 | tf_op jit(solution)/shard_map/ppermute | solution.py:128
  562.9 27.6 %collective-permute-done.30 = bf16[2,128,1536]{2,1,0:T(8,128)(2,1)S(1)} collective-permute-done((bf16[2,128,1536]{2,1,0:T(8,128)(2,1)S(1)}, bf16[2,128,1536]{2,1,0:T(8,128)(2,1)S(1)}, u32[]{:S(2)}, u32[]{:S(2)}) %collective-permute-start.30) | collective-permute-done | bytes 786464 | tf_op jit(solution)/shard_map/ppermute | solution.py:128
  595.3 12.1 %collective-permute-done.19 = bf16[2,128,1536]{2,1,0:T(8,128)(2,1)S(1)} collective-permute-done((bf16[2,128,1536]{2,1,0:T(8,128)(2,1)S(1)}, bf16[2,128,1536]{2,1,0:T(8,128)(2,1)S(1)}, u32[]{:S(2)}, u32[]{:S(2)}) %collective-permute-start.19) | collective-permute-done | bytes 786464 | tf_op jit(solution)/shard_map/ppermute | solution.py:128
  609.0 15.2 %collective-permute-done.29 = bf16[2,128,1536]{2,1,0:T(8,128)(2,1)S(1)} collective-permute-done((bf16[2,128,1536]{2,1,0:T(8,128)(2,1)S(1)}, bf16[2,128,1536]{2,1,0:T(8,128)(2,1)S(1)}, u32[]{:S(2)}, u32[]{:S(2)}) %collective-permute-start.29) | collective-permute-done | bytes 786464 | tf_op jit(solution)/shard_map/ppermute | solution.py:128
  627.2 16.4 %collective-permute-done.35 = bf16[2,128,1536]{2,1,0:T(8,128)(2,1)S(1)} collective-permute-done((bf16[2,128,1536]{2,1,0:T(8,128)(2,1)S(1)}, bf16[2,128,1536]{2,1,0:T(8,128)(2,1)S(1)}, u32[]{:S(2)}, u32[]{:S(2)}) %collective-permute-start.35) | collective-permute-done | bytes 786464 | tf_op jit(solution)/shard_map/ppermute | solution.py:128
  664.3 30.5 %collective-permute-done.36 = bf16[128,1536]{1,0:T(8,128)(2,1)S(1)} collective-permute-done((bf16[128,1536]{1,0:T(8,128)(2,1)S(1)}, bf16[128,1536]{1,0:T(8,128)(2,1)S(1)}, u32[]{:S(2)}, u32[]{:S(2)}) %collective-permute-start.36) | collective-permute-done | bytes 393248 | tf_op jit(solution)/shard_map/ppermute | solution.py:128
  696.0 15.6 %collective-permute-done.26 = bf16[128,1536]{1,0:T(8,128)(2,1)S(1)} collective-permute-done((bf16[128,1536]{1,0:T(8,128)(2,1)S(1)}, bf16[128,1536]{1,0:T(8,128)(2,1)S(1)}, u32[]{:S(2)}, u32[]{:S(2)}) %collective-permute-start.26) | collective-permute-done | bytes 393248 | tf_op jit(solution)/shard_map/ppermute | solution.py:128
  714.9 48.6 %while.30 = (s32[]{:T(128)}, f32[8,3,128,64]{2,3,1,0:T(8,128)}, f32[8,128,64]{1,2,0:T(8,128)S(1)}, bf16[8,128,64]{1,2,0:T(8,128)(2,1)}, bf16[8,3,128,64]{2,3,1,0...) while((s32[]{:T(128)}, f32[8,3,128,64]{2,3,1,0:T(8,128)}, ...), condition=%wide.region_12.13_spmd.clone, body=%wide.region_10.12_spmd.clone.sunk | while | flops 31981184 | bytes 1439357 | solution.py:594
  786.4 21.2 %take_blocks.2 = bf16[32,48,2688]{2,1,0:T(8,128)(2,1)} custom-call(s32[32]{0:T(128)} %get-tuple-element.317.order_ref, f32[32,48,2560]{2,1,0:T(8,128)} %bitcast.245, f32[32,48,128]{2,1,0:T(8,128)} %maximum_maximum_fusion.refs_1_), custom_call_target="tpu_custom_call" | custom-call | tf_op jit(solution)/shard_map/take_blocks/pallas_call | solution.py:208
  817.2 19.4 %take_blocks.3 = bf16[32,48,1536]{2,1,0:T(8,128)(2,1)} custom-call(s32[32]{0:T(128)} %get-tuple-element.317.order_ref, f32[32,48,1536]{2,1,0:T(8,128)} %fusion.86.refs_0_), custom_call_target="tpu_custom_call" | custom-call | tf_op jit(solution)/shard_map/take_blocks/pallas_call | solution.py:208
  857.1 10.0 %unpack_units.1 = f32[10,192,1536]{2,1,0:T(8,128)} custom-call(bf16[40,192,384]{2,1,0:T(8,128)(2,1)} %bitcast.65.u_ref), custom_call_target="tpu_custom_call" | custom-call | tf_op jit(solution)/shard_map/unpack_units/pallas_call | solution.py:255
  895.1 9.9 %collective-permute-done.45 = bf16[2,48,2688]{2,1,0:T(8,128)(2,1)S(1)} collective-permute-done((bf16[2,48,2688]{2,1,0:T(8,128)(2,1)S(1)}, bf16[2,48,2688]{2,1,0:T(8,128)(2,1)S(1)}, u32[]{:S(2)}, u32[]{:S(2)}) %collective-permute-start.45) | collective-permute-done | bytes 516128 | tf_op jit(solution)/shard_map/ppermute | solution.py:128
  918.3 13.0 %collective-permute-done.46 = bf16[48,2688]{1,0:T(8,128)(2,1)S(1)} collective-permute-done((bf16[48,2688]{1,0:T(8,128)(2,1)S(1)}, bf16[48,2688]{1,0:T(8,128)(2,1)S(1)}, u32[]{:S(2)}, u32[]{:S(2)}) %collective-permute-start.46) | collective-permute-done | bytes 258080 | tf_op jit(solution)/shard_map/ppermute | solution.py:128
  (404 shorter events, 312.9 us)
Async XLA Ops:
  7.2 214.6 %all-gather.3.cloned.1.call-start = ((), (), s32[]{:S(2)}) async-start(), calls=%async_computation.3 | async-start | bytes 8515584 | tf_op jit(solution)/shard_map/all_gather | solution.py:522
  26.4 358.6 %all-to-all-start = ((bf16[8,5,192,384]{3,2,1,0:T(8,128)(2,1)}), bf16[8,5,192,384]{3,2,1,0:T(8,128)(2,1)}, u32[]{:S(2)}, u32[]{:S(2)}) async-start(bf16[8,5,192,384]{3,2,1,0:T(8,128)(2,1)} %bitcast.246), calls=%async_computation | async-start | bytes 11796480 | tf_op jit(solution)/shard_map/all_to_all | solution.py:532
  32.5 254.8 %all-gather.5.cloned.1.call-start = ((), (), s32[]{:S(2)}) async-start(), calls=%async_computation.4 | async-start | bytes 4866048 | tf_op jit(solution)/shard_map/all_gather | solution.py:523
  50.4 249.1 %collective-permute-start.13 = (bf16[4,128,1536]{2,1,0:T(8,128)(2,1)}, bf16[4,128,1536]{2,1,0:T(8,128)(2,1)}, u32[]{:S(2)}, u32[]{:S(2)}) collective-permute-start(bf16[4,128,1536]{2,1,0:T(8,128)(2,1)} %pad_maximum_fusion.1), channel_id=1, source_target_pairs={{0,16},{1,17},{2,18},{3,19},{4,20},{5,21},{6,22},{7,23},{8,24},{9,... | collective-permute-start | bytes 4718600 | tf_op jit(solution)/shard_map/ppermute | solution.py:128
  52.0 244.9 %collective-permute-start.12 = (bf16[4,128,1536]{2,1,0:T(8,128)(2,1)}, bf16[4,128,1536]{2,1,0:T(8,128)(2,1)}, u32[]{:S(2)}, u32[]{:S(2)}) collective-permute-start(bf16[4,128,1536]{2,1,0:T(8,128)(2,1)} %pad_maximum_fusion.1), channel_id=1, source_target_pairs={{0,1},{1,0},{2,3},{3,2},{4,5},{5,4},{6,7},{7,6},{8,9},{9,8},{10,11... | collective-permute-start | bytes 4718600 | tf_op jit(solution)/shard_map/ppermute | solution.py:128
  310.4 74.6 %collective-permute-start.16 = (bf16[8,128,1536]{2,1,0:T(8,128)(2,1)}, bf16[8,128,1536]{2,1,0:T(8,128)(2,1)}, u32[]{:S(2)}, u32[]{:S(2)}) collective-permute-start(bf16[8,128,1536]{2,1,0:T(8,128)(2,1)} %constant_dynamic-update-slice_fusion.8.c0), channel_id=1, source_target_pairs={{0,8},{1,9},{2,10},{3,11},{4,12},{5,13},{6,14},{7,15},{8,0},{9,1},... | collective-permute-start | bytes 9437192 | tf_op jit(solution)/shard_map/ppermute | solution.py:128
  328.1 37.3 %collective-permute-start.4 = (bf16[4,128,1536]{2,1,0:T(8,128)(2,1)S(1)}, bf16[4,128,1536]{2,1,0:T(8,128)(2,1)S(1)}, u32[]{:S(2)}, u32[]{:S(2)}) collective-permute-start(bf16[4,128,1536]{2,1,0:T(8,128)(2,1)S(1)} %pad_maximum_fusion), channel_id=1, source_target_pairs={{0,16},{1,17},{2,18},{3,19},{4,20},{5,21},{6,22},{7,23},{8,24},{9,... | collective-permute-start | bytes 4718600 | tf_op jit(solution)/shard_map/ppermute | solution.py:128
  329.7 55.3 %collective-permute-start.17 = (bf16[8,128,1536]{2,1,0:T(8,128)(2,1)}, bf16[8,128,1536]{2,1,0:T(8,128)(2,1)}, u32[]{:S(2)}, u32[]{:S(2)}) collective-permute-start(bf16[8,128,1536]{2,1,0:T(8,128)(2,1)} %constant_dynamic-update-slice_fusion.13.c1), channel_id=1, source_target_pairs={{0,8},{1,9},{2,10},{3,11},{4,12},{5,13},{6,14},{7,15},{8,0},{9,1},... | collective-permute-start | bytes 9437192 | tf_op jit(solution)/shard_map/ppermute | solution.py:128
  459.1 39.1 %collective-permute-start.28 = (bf16[16,128,1536]{2,1,0:T(8,128)(2,1)}, bf16[16,128,1536]{2,1,0:T(8,128)(2,1)}, u32[]{:S(2)}, u32[]{:S(2)}) collective-permute-start(bf16[16,128,1536]{2,1,0:T(8,128)(2,1)} %get-tuple-element.128), channel_id=1, source_target_pairs={{0,8},{1,9},{2,10},{3,11},{4,12},{5,13},{6,14},{7,15},{8,0},{9,1},... | collective-permute-start | bytes 18874376 | tf_op jit(solution)/shard_map/ppermute | solution.py:128
  481.3 375.8 %all-to-all-start.2 = ((bf16[8,5,192,384]{3,2,1,0:T(8,128)(2,1)}), bf16[8,5,192,384]{3,2,1,0:T(8,128)(2,1)}, u32[]{:S(2)}, u32[]{:S(2)}) async-start(bf16[8,5,192,384]{3,2,1,0:T(8,128)(2,1)} %get-tuple-element.133), calls=%async_computation.2 | async-start | bytes 11796480 | tf_op jit(solution)/shard_map/all_to_all | solution.py:622
  494.7 63.6 %collective-permute-start.20 = (bf16[2,128,1536]{2,1,0:T(8,128)(2,1)S(1)}, bf16[2,128,1536]{2,1,0:T(8,128)(2,1)S(1)}, u32[]{:S(2)}, u32[]{:S(2)}) collective-permute-start(bf16[2,128,1536]{2,1,0:T(8,128)(2,1)S(1)} %get-tuple-element.277), channel_id=1, source_target_pairs={{0,1},{1,0},{2,3},{3,2},{4,5},{5,4},{6,7},{7,6},{8,9},{9,8},{10,11... | collective-permute-start | bytes 2359304 | tf_op jit(solution)/shard_map/ppermute | solution.py:128
  496.7 61.5 %collective-permute-start.23 = (bf16[2,128,1536]{2,1,0:T(8,128)(2,1)S(1)}, bf16[2,128,1536]{2,1,0:T(8,128)(2,1)S(1)}, u32[]{:S(2)}, u32[]{:S(2)}) collective-permute-start(bf16[2,128,1536]{2,1,0:T(8,128)(2,1)S(1)} %get-tuple-element.275), channel_id=1, source_target_pairs={{0,16},{1,17},{2,18},{3,19},{4,20},{5,21},{6,22},{7,23},{8,24},{9,... | collective-permute-start | bytes 2359304 | tf_op jit(solution)/shard_map/ppermute | solution.py:128
  501.4 89.2 %collective-permute-start.30 = (bf16[2,128,1536]{2,1,0:T(8,128)(2,1)S(1)}, bf16[2,128,1536]{2,1,0:T(8,128)(2,1)S(1)}, u32[]{:S(2)}, u32[]{:S(2)}) collective-permute-start(bf16[2,128,1536]{2,1,0:T(8,128)(2,1)S(1)} %get-tuple-element.269), channel_id=1, source_target_pairs={{0,1},{1,0},{2,3},{3,2},{4,5},{5,4},{6,7},{7,6},{8,9},{9,8},{10,11... | collective-permute-start | bytes 2359304 | tf_op jit(solution)/shard_map/ppermute | solution.py:128
  501.5 89.0 %collective-permute-start.33 = (bf16[2,128,1536]{2,1,0:T(8,128)(2,1)S(1)}, bf16[2,128,1536]{2,1,0:T(8,128)(2,1)S(1)}, u32[]{:S(2)}, u32[]{:S(2)}) collective-permute-start(bf16[2,128,1536]{2,1,0:T(8,128)(2,1)S(1)} %get-tuple-element.267), channel_id=1, source_target_pairs={{0,16},{1,17},{2,18},{3,19},{4,20},{5,21},{6,22},{7,23},{8,24},{9,... | collective-permute-start | bytes 2359304 | tf_op jit(solution)/shard_map/ppermute | solution.py:128
  502.5 104.9 %collective-permute-start.19 = (bf16[2,128,1536]{2,1,0:T(8,128)(2,1)S(1)}, bf16[2,128,1536]{2,1,0:T(8,128)(2,1)S(1)}, u32[]{:S(2)}, u32[]{:S(2)}) collective-permute-start(bf16[2,128,1536]{2,1,0:T(8,128)(2,1)S(1)} %get-tuple-element.278), channel_id=1, source_target_pairs={{0,1},{1,0},{2,3},{3,2},{4,5},{5,4},{6,7},{7,6},{8,9},{9,8},{10,11... | collective-permute-start | bytes 2359304 | tf_op jit(solution)/shard_map/ppermute | solution.py:128
  558.3 66.0 %collective-permute-start.29 = (bf16[2,128,1536]{2,1,0:T(8,128)(2,1)S(1)}, bf16[2,128,1536]{2,1,0:T(8,128)(2,1)S(1)}, u32[]{:S(2)}, u32[]{:S(2)}) collective-permute-start(bf16[2,128,1536]{2,1,0:T(8,128)(2,1)S(1)} %get-tuple-element.270), channel_id=1, source_target_pairs={{0,1},{1,0},{2,3},{3,2},{4,5},{5,4},{6,7},{7,6},{8,9},{9,8},{10,11... | collective-permute-start | bytes 2359304 | tf_op jit(solution)/shard_map/ppermute | solution.py:128
  560.7 48.1 %collective-permute-start.21 = (bf16[2,128,1536]{2,1,0:T(8,128)(2,1)S(1)}, bf16[2,128,1536]{2,1,0:T(8,128)(2,1)S(1)}, u32[]{:S(2)}, u32[]{:S(2)}) collective-permute-start(bf16[2,128,1536]{2,1,0:T(8,128)(2,1)S(1)} %get-tuple-element.279), channel_id=1, source_target_pairs={{0,16},{1,17},{2,18},{3,19},{4,20},{5,21},{6,22},{7,23},{8,24},{9,... | collective-permute-start | bytes 2359304 | tf_op jit(solution)/shard_map/ppermute | solution.py:128
  594.7 53.9 %collective-permute-start.25 = (bf16[2,128,1536]{2,1,0:T(8,128)(2,1)S(1)}, bf16[2,128,1536]{2,1,0:T(8,128)(2,1)S(1)}, u32[]{:S(2)}, u32[]{:S(2)}) collective-permute-start(bf16[2,128,1536]{2,1,0:T(8,128)(2,1)S(1)} %get-tuple-element.274), channel_id=1, source_target_pairs={{0,16},{1,17},{2,18},{3,19},{4,20},{5,21},{6,22},{7,23},{8,24},{9,... | collective-permute-start | bytes 2359304 | tf_op jit(solution)/shard_map/ppermute | solution.py:128
  608.9 38.9 %collective-permute-start.34 = (bf16[2,128,1536]{2,1,0:T(8,128)(2,1)S(1)}, bf16[2,128,1536]{2,1,0:T(8,128)(2,1)S(1)}, u32[]{:S(2)}, u32[]{:S(2)}) collective-permute-start(bf16[2,128,1536]{2,1,0:T(8,128)(2,1)S(1)} %get-tuple-element.272), channel_id=1, source_target_pairs={{0,1},{1,0},{2,3},{3,2},{4,5},{5,4},{6,7},{7,6},{8,9},{9,8},{10,11... | collective-permute-start | bytes 2359304 | tf_op jit(solution)/shard_map/ppermute | solution.py:128
  624.3 71.7 %collective-permute-start.22 = (bf16[128,1536]{1,0:T(8,128)(2,1)S(1)}, bf16[128,1536]{1,0:T(8,128)(2,1)S(1)}, u32[]{:S(2)}, u32[]{:S(2)}) collective-permute-start(bf16[128,1536]{1,0:T(8,128)(2,1)S(1)} %fusion.79), channel_id=1, source_target_pairs={{0,2},{1,3},{2,0},{3,1},{4,6},{5,7},{6,4},{7,5},{8,10},{9,11},{10,... | collective-permute-start | bytes 1179656 | tf_op jit(solution)/shard_map/ppermute | solution.py:128
  648.1 46.7 %collective-permute-start.36 = (bf16[128,1536]{1,0:T(8,128)(2,1)S(1)}, bf16[128,1536]{1,0:T(8,128)(2,1)S(1)}, u32[]{:S(2)}, u32[]{:S(2)}) collective-permute-start(bf16[128,1536]{1,0:T(8,128)(2,1)S(1)} %get-tuple-element.297), channel_id=1, source_target_pairs={{0,4},{1,5},{2,6},{3,7},{4,0},{5,1},{6,2},{7,3},{8,12},{9,13},{10,... | collective-permute-start | bytes 1179656 | tf_op jit(solution)/shard_map/ppermute | solution.py:128
  648.6 46.1 %collective-permute-start.37 = (bf16[128,1536]{1,0:T(8,128)(2,1)S(1)}, bf16[128,1536]{1,0:T(8,128)(2,1)S(1)}, u32[]{:S(2)}, u32[]{:S(2)}) collective-permute-start(bf16[128,1536]{1,0:T(8,128)(2,1)S(1)} %get-tuple-element.298), channel_id=1, source_target_pairs={{0,6},{1,7},{2,4},{3,5},{4,2},{5,3},{6,0},{7,1},{8,14},{9,15},{10,... | collective-permute-start | bytes 1179656 | tf_op jit(solution)/shard_map/ppermute | solution.py:128
  657.1 54.5 %collective-permute-start.26 = (bf16[128,1536]{1,0:T(8,128)(2,1)S(1)}, bf16[128,1536]{1,0:T(8,128)(2,1)S(1)}, u32[]{:S(2)}, u32[]{:S(2)}) collective-permute-start(bf16[128,1536]{1,0:T(8,128)(2,1)S(1)} %get-tuple-element.299), channel_id=1, source_target_pairs={{0,4},{1,5},{2,6},{3,7},{4,0},{5,1},{6,2},{7,3},{8,12},{9,13},{10,... | collective-permute-start | bytes 1179656 | tf_op jit(solution)/shard_map/ppermute | solution.py:128
  662.0 49.6 %collective-permute-start.27 = (bf16[128,1536]{1,0:T(8,128)(2,1)S(1)}, bf16[128,1536]{1,0:T(8,128)(2,1)S(1)}, u32[]{:S(2)}, u32[]{:S(2)}) collective-permute-start(bf16[128,1536]{1,0:T(8,128)(2,1)S(1)} %get-tuple-element.300), channel_id=1, source_target_pairs={{0,6},{1,7},{2,4},{3,5},{4,2},{5,3},{6,0},{7,1},{8,14},{9,15},{10,... | collective-permute-start | bytes 1179656 | tf_op jit(solution)/shard_map/ppermute | solution.py:128
  (75 other events, 2074.7 us)
Sparse Core Ops, SparseCore 0:
  12.2 209.4 all-gather.2
  224.7 62.5 all-gather.4
